TPU v7x, 512 devices: a whole 4x8x8 slice. The times are simulated.
512 devices in a mesh: pipe: 32 (over z_hi, y), dp: 16 (over x, z_lo, core).
Axes of the slice: x: 4, y: 8, z: 8 (z_hi: 4, z_lo: 2; z = z_hi * 2 + z_lo), core: 2. Of those that a mesh axis runs over, the one named last changes fastest.
Arguments:
- section_inputs: bfloat16 [32, 3072, 6144], P('pipe', 'dp'), may hold values from -6 to 6
- loss_grad: bfloat16 [3072, 6144], P('dp', 'pipe'), may hold values from -6 to 6
- weight_blocks: bfloat16 [32, 48, 128, 128], P('pipe', 'dp'), may hold values from -0.3125 to 0.3125
- left_factor: bfloat16 [32, 6144, 64], P('pipe', 'dp'), may hold values from -0.078125 to 0.078125
- right_factor: bfloat16 [32, 64, 6144], P('pipe', None, 'dp'), may hold values from -0.5 to 0.5
- block_column: int32 [32, 48], P('pipe'), may hold values from 0 to 47, each once within a row
- live_length: int32 [16, 12], P('dp'), may hold values from 1 to 16, 144 in all within a row
Outputs:
- in_grad: bfloat16 [32, 3072, 6144], P('pipe', 'dp')
- grad_blocks: bfloat16 [32, 48, 128, 128], P('pipe', 'dp')
- grad_left: bfloat16 [32, 6144, 64], P('pipe', 'dp')
- grad_right: bfloat16 [32, 64, 6144], P('pipe', None, 'dp')
Inputs may be any that keep to these rules, and one draw needn't show every extreme that they name: `block_column`: each section's row is a permutation of 0 to 47. `live_length`: each row sums to 144 live tokens.
All inputs are finite; a program needn't handle non-finite values.
Results may differ from a plain program's by a relative error of at most 0.035.
Values may be sent and summed in bfloat16 or wider, within the bound.
A program may use at most 64 MiB of HBM per device.

v0:
```python
import math
import jax
import jax.numpy as jnp
from jax import lax
from jax.sharding import PartitionSpec as P


def shifted(shard, axis, by):
    count = lax.axis_size(axis)
    pairs = [(i, i + by) for i in range(count) if 0 <= i + by < count]
    return lax.ppermute(shard, axis, pairs)


def slope_of(values):
    cumulative = 0.5 * (1.0 + jax.scipy.special.erf(values * (1.0 / math.sqrt(2.0))))
    density = jnp.exp(-0.5 * values * values) * (1.0 / math.sqrt(2.0 * math.pi))
    return cumulative + values * density


def inverse_of(columns):
    number = columns.shape[0]
    ladder = jnp.arange(number, dtype=jnp.int32)
    matches = (columns[:, None] == ladder[None, :]).astype(jnp.int32)
    return jnp.sum(matches * ladder[:, None], axis=0)


def section_rows(inputs, incoming, blocks, left_whole, right_whole, columns, inverse):
    row_count, features = inputs.shape
    number, block_size = (blocks.shape[0], blocks.shape[1])
    split_in = inputs.reshape(row_count, number, block_size)
    sparse = jnp.einsum("tnb,nbc->tnc", split_in, blocks, preferred_element_type=jnp.float32)
    sparse = jnp.take(sparse, inverse, axis=1).reshape(row_count, features)
    lowered = jnp.dot(inputs, left_whole, preferred_element_type=jnp.float32).astype(jnp.bfloat16)
    preactivation = sparse + jnp.dot(lowered, right_whole, preferred_element_type=jnp.float32)
    delta_grad = (incoming.astype(jnp.float32) * slope_of(preactivation)).astype(jnp.bfloat16)
    delta_split = jnp.take(delta_grad.reshape(row_count, number, block_size), columns, axis=1)
    back_sparse = jnp.einsum(
        "tnc,nbc->tnb", delta_split, blocks, preferred_element_type=jnp.float32
    ).reshape(row_count, features)
    reduced = jnp.einsum(
        "td,rd->tr", delta_grad, right_whole, preferred_element_type=jnp.float32
    ).astype(jnp.bfloat16)
    back_low = jnp.einsum("tr,dr->td", reduced, left_whole, preferred_element_type=jnp.float32)
    outgoing = (incoming.astype(jnp.float32) + back_sparse + back_low).astype(jnp.bfloat16)
    return (outgoing, delta_split, lowered, reduced)


def weight_terms(inputs, delta_split, lowered, reduced):
    row_count, features = inputs.shape
    number, block_size = (delta_split.shape[1], delta_split.shape[2])
    split_in = inputs.reshape(row_count, number, block_size)
    grad_blocks = jnp.einsum(
        "tnb,tnc->nbc", split_in, delta_split, preferred_element_type=jnp.float32
    )
    grad_left = jnp.einsum("td,tr->dr", inputs, reduced, preferred_element_type=jnp.float32)
    grad_mixed = jnp.einsum("tr,tnc->rnc", lowered, delta_split, preferred_element_type=jnp.float32)
    return (grad_blocks, grad_left, grad_mixed)


def replace_rows(buffer, fresh, start, active):
    older = lax.dynamic_slice_in_dim(buffer, start, fresh.shape[0], 0)
    return lax.dynamic_update_slice_in_dim(buffer, jnp.where(active, fresh, older), start, 0)


def body(
    section_inputs, loss_grad, weight_blocks, left_factor, right_factor, block_column, live_length
):
    inputs = section_inputs[0]
    blocks, left_whole, right_whole = (
        lax.all_gather(weight_blocks[0], "dp", axis=0, tiled=True),
        lax.all_gather(left_factor[0], "dp", axis=0, tiled=True),
        lax.all_gather(right_factor[0], "dp", axis=1, tiled=True),
    )
    head = lax.all_gather(loss_grad, "pipe", axis=1, tiled=True)
    columns = block_column[0]
    inverse = inverse_of(columns)
    sections = lax.axis_size("pipe")
    section = lax.axis_index("pipe")
    token_count, features = inputs.shape
    micro_count = live_length.shape[1]
    micro_rows = token_count // micro_count
    number, block_size = (blocks.shape[0], blocks.shape[1])
    rank_width = left_whole.shape[1]
    positions = jnp.arange(token_count, dtype=jnp.int32)
    owners = (positions // micro_rows)[:, None] == jnp.arange(micro_count, dtype=jnp.int32)[None, :]
    limits = jnp.sum(jnp.where(owners, live_length[0][None, :], 0), axis=1)
    live_rows = positions % micro_rows < limits
    seeded = jnp.where(live_rows[:, None], head, jnp.zeros_like(head))
    work_count = inputs.shape[0]
    turns = micro_count + sections - 1
    stored = (
        jnp.zeros((work_count, number, block_size), jnp.bfloat16),
        jnp.zeros((work_count, rank_width), jnp.bfloat16),
        jnp.zeros((work_count, rank_width), jnp.bfloat16),
    )

    def compute(upstream, rows_in):
        return section_rows(rows_in, upstream, blocks, left_whole, right_whole, columns, inverse)

    def skipped(upstream, rows_in):
        return (
            jnp.zeros_like(upstream),
            jnp.zeros((micro_rows, number, block_size), jnp.bfloat16),
            jnp.zeros((micro_rows, rank_width), jnp.bfloat16),
            jnp.zeros((micro_rows, rank_width), jnp.bfloat16),
        )

    def turn(index, carry):
        incoming, grads_out, saved = carry
        micro = index - (sections - 1 - section)
        active = (micro >= 0) & (micro < micro_count)
        start = jnp.clip(micro, 0, micro_count - 1) * micro_rows
        rows_in = lax.dynamic_slice_in_dim(inputs, start, micro_rows, 0)
        from_head = lax.dynamic_slice_in_dim(seeded, start, micro_rows, 0)
        upstream = jnp.where(section == sections - 1, from_head, incoming)
        outgoing, delta_split, lowered, reduced = lax.cond(
            active, compute, skipped, upstream, rows_in
        )
        grads_out = replace_rows(grads_out, outgoing, start, active)
        saved = (
            replace_rows(saved[0], delta_split, start, active),
            replace_rows(saved[1], lowered, start, active),
            replace_rows(saved[2], reduced, start, active),
        )
        passed = shifted(outgoing, "pipe", -1)
        return (passed, grads_out, saved)

    start_grad = jnp.zeros((micro_rows, features), jnp.bfloat16)
    unused, work_grad, saved = lax.fori_loop(
        0, turns, turn, (start_grad, jnp.zeros_like(inputs), stored)
    )
    grad_blocks, grad_left, grad_mixed = weight_terms(inputs, saved[0], saved[1], saved[2])
    grad_right = jnp.take(grad_mixed, inverse, axis=1).reshape(rank_width, features)
    sum_blocks, sum_left, sum_right = (
        lax.psum_scatter(
            grad_blocks.astype(jnp.bfloat16), "dp", scatter_dimension=0, tiled=True
        ).astype(jnp.float32),
        lax.psum_scatter(
            grad_left.astype(jnp.bfloat16), "dp", scatter_dimension=0, tiled=True
        ).astype(jnp.float32),
        lax.psum_scatter(
            grad_right.astype(jnp.bfloat16), "dp", scatter_dimension=1, tiled=True
        ).astype(jnp.float32),
    )
    return (
        work_grad[None],
        sum_blocks.astype(jnp.bfloat16)[None],
        sum_left.astype(jnp.bfloat16)[None],
        sum_right.astype(jnp.bfloat16)[None],
    )


def solution(mesh):
    in_specs = (
        P("pipe", "dp", None),
        P("dp", "pipe"),
        P("pipe", "dp", None, None),
        P("pipe", "dp", None),
        P("pipe", None, "dp"),
        P("pipe", None),
        P("dp", None),
    )
    out_specs = (
        P("pipe", "dp", None),
        P("pipe", "dp", None, None),
        P("pipe", "dp", None),
        P("pipe", None, "dp"),
    )
    return jax.shard_map(body, mesh=mesh, in_specs=in_specs, out_specs=out_specs, check_vma=False)
```

profile of v0, /device:TPU:8, one launch (start us, length us, event | category | flops | bytes accessed | tf_op | source)
XLA Modules:
  0.0 1399.3 jit_solution(17293354459489336557)
XLA Ops:
  15.0 29.2 %all-gather.1 = bf16[1,6144,64]{2,1,0:T(8,128)(2,1)S(1)} all-gather(bf16[1,384,64]{2,1,0:T(8,128)(2,1)S(1)} %copy.44), channel_id=3, replica_groups=mesh['pipe'=32,'dp'=16] {'dp'}, dimensions={1}, use_global_device_ids=true | all-gather | bytes 835584 | tf_op jit(solution)/shard_map/all_gather | solution.py:71
  44.2 23.6 %all-gather.2 = bf16[1,64,6144]{2,1,0:T(8,128)(2,1)} all-gather(bf16[1,64,384]{2,1,0:T(8,128)(2,1)} %param.15), channel_id=4, replica_groups=mesh['pipe'=32,'dp'=16] {'dp'}, dimensions={2}, use_global_device_ids=true | all-gather | bytes 835584 | tf_op jit(solution)/shard_map/all_gather | solution.py:72
  67.8 41.7 %all-gather.6.cloned.1.call-done = bf16[192,6144]{0,1:T(8,128)(2,1)} async-done(((bf16[192,192]{0,1:T(8,128)(2,1)}), bf16[192,6144]{0,1:T(8,128)(2,1)}) %all-gather.6.cloned.1.call-update) | async-done | bytes 2359312 | tf_op jit(solution)/shard_map/all_gather | solution.py:74
  113.3 4.6 copy.46
  117.9 28.8 %all-gather.8.cloned.1.call-done = bf16[1,48,128,128]{3,2,0,1:T(8,128)(2,1)} async-done(((bf16[1,3,128,128]{3,2,0,1:T(8,128)(2,1)}), bf16[1,48,128,128]{3,2,0,1:T(8,128)(2,1)}) %all-gather.8.cloned.1.call-update) | async-done | bytes 1572880 | tf_op jit(solution)/shard_map/all_gather | solution.py:70
  152.3 1034.6 %while.23 = (s32[]{:T(128)}, bf16[16,6144]{1,0:T(8,128)(2,1)}, bf16[192,6144]{1,0:T(8,128)(2,1)}, bf16[192,48,128]{2,0,1:T(8,128)(2,1)}, bf16[192,64]{1,0:T(8,12...) while((s32[]{:T(128)}, bf16[16,6144]{1,0:T(8,128)(2,1)}, ...), condition=%wide.region_5.6_spmd, body=%wide.region_2.5_spmd.sunk | while | flops 102833008 | bytes 20126928 | solution.py:129
  252.7 6.2 collective-permute-done
  268.1 5.0 collective-permute-done
  295.2 5.9 collective-permute-done
  310.4 6.2 collective-permute-done
  325.9 5.6 collective-permute-done
  340.9 5.2 collective-permute-done
  355.4 5.2 collective-permute-done
  396.0 4.2 collective-permute-done
  409.5 4.6 collective-permute-done
  423.4 6.6 collective-permute-done
  439.3 8.9 collective-permute-done
  457.5 7.8 collective-permute-done
  474.6 5.2 collective-permute-done
  502.1 5.1 collective-permute-done
  553.0 272.2 %collective-permute-done = bf16[16,6144]{1,0:T(8,128)(2,1)S(1)} collective-permute-done((bf16[16,6144]{1,0:T(8,128)(2,1)}, bf16[16,6144]{1,0:T(8,128)(2,1)S(1)}, u32[]{:S(2)}, u32[]{:S(2)}) %collective-permute-start) | collective-permute-done | bytes 196640 | tf_op jit(solution)/shard_map/while/body/eval_jaxpr/ppermute | solution.py:11
  825.8 14.4 %conditional.2 = (bf16[16,6144]{1,0:T(8,128)(2,1)}, bf16[16,48,128]{2,0,1:T(8,128)(2,1)}, bf16[16,64]{1,0:T(8,128)(2,1)S(1)}, bf16[16,64]{1,0:T(8,128)(2,1)}) conditional(s32[]{:T(128)} %convert_element_type.80, () %tuple.65, (pred[]{:T(512)}, bf16[192,6144]{1,0:T(8,128)(2,1)}, s32[]{:T(128)}, bf16[16,6144]{1,0:T(8,128)(2,1)}, s32[48]{0:T(128)}, ...), branch_computations={%region_3.3_spmd, %region_4.4_spmd} | conditional | flops 102634336 | bytes 17349906 | solution.py:116
  847.1 5.8 collective-permute-done
  853.6 14.4 %conditional.2 = (bf16[16,6144]{1,0:T(8,128)(2,1)}, bf16[16,48,128]{2,0,1:T(8,128)(2,1)}, bf16[16,64]{1,0:T(8,128)(2,1)S(1)}, bf16[16,64]{1,0:T(8,128)(2,1)}) conditional(s32[]{:T(128)} %convert_element_type.80, () %tuple.65, (pred[]{:T(512)}, bf16[192,6144]{1,0:T(8,128)(2,1)}, s32[]{:T(128)}, bf16[16,6144]{1,0:T(8,128)(2,1)}, s32[48]{0:T(128)}, ...), branch_computations={%region_3.3_spmd, %region_4.4_spmd} | conditional | flops 102634336 | bytes 17349906 | solution.py:116
  874.8 6.3 collective-permute-done
  881.8 14.4 %conditional.2 = (bf16[16,6144]{1,0:T(8,128)(2,1)}, bf16[16,48,128]{2,0,1:T(8,128)(2,1)}, bf16[16,64]{1,0:T(8,128)(2,1)S(1)}, bf16[16,64]{1,0:T(8,128)(2,1)}) conditional(s32[]{:T(128)} %convert_element_type.80, () %tuple.65, (pred[]{:T(512)}, bf16[192,6144]{1,0:T(8,128)(2,1)}, s32[]{:T(128)}, bf16[16,6144]{1,0:T(8,128)(2,1)}, s32[48]{0:T(128)}, ...), branch_computations={%region_3.3_spmd, %region_4.4_spmd} | conditional | flops 102634336 | bytes 17349906 | solution.py:116
  903.0 8.3 collective-permute-done
  912.0 14.4 %conditional.2 = (bf16[16,6144]{1,0:T(8,128)(2,1)}, bf16[16,48,128]{2,0,1:T(8,128)(2,1)}, bf16[16,64]{1,0:T(8,128)(2,1)S(1)}, bf16[16,64]{1,0:T(8,128)(2,1)}) conditional(s32[]{:T(128)} %convert_element_type.80, () %tuple.65, (pred[]{:T(512)}, bf16[192,6144]{1,0:T(8,128)(2,1)}, s32[]{:T(128)}, bf16[16,6144]{1,0:T(8,128)(2,1)}, s32[48]{0:T(128)}, ...), branch_computations={%region_3.3_spmd, %region_4.4_spmd} | conditional | flops 102634336 | bytes 17349906 | solution.py:116
  933.2 8.3 collective-permute-done
  942.2 14.4 %conditional.2 = (bf16[16,6144]{1,0:T(8,128)(2,1)}, bf16[16,48,128]{2,0,1:T(8,128)(2,1)}, bf16[16,64]{1,0:T(8,128)(2,1)S(1)}, bf16[16,64]{1,0:T(8,128)(2,1)}) conditional(s32[]{:T(128)} %convert_element_type.80, () %tuple.65, (pred[]{:T(512)}, bf16[192,6144]{1,0:T(8,128)(2,1)}, s32[]{:T(128)}, bf16[16,6144]{1,0:T(8,128)(2,1)}, s32[48]{0:T(128)}, ...), branch_computations={%region_3.3_spmd, %region_4.4_spmd} | conditional | flops 102634336 | bytes 17349906 | solution.py:116
  963.4 6.8 collective-permute-done
  970.9 14.4 %conditional.2 = (bf16[16,6144]{1,0:T(8,128)(2,1)}, bf16[16,48,128]{2,0,1:T(8,128)(2,1)}, bf16[16,64]{1,0:T(8,128)(2,1)S(1)}, bf16[16,64]{1,0:T(8,128)(2,1)}) conditional(s32[]{:T(128)} %convert_element_type.80, () %tuple.65, (pred[]{:T(512)}, bf16[192,6144]{1,0:T(8,128)(2,1)}, s32[]{:T(128)}, bf16[16,6144]{1,0:T(8,128)(2,1)}, s32[48]{0:T(128)}, ...), branch_computations={%region_3.3_spmd, %region_4.4_spmd} | conditional | flops 102634336 | bytes 17349906 | solution.py:116
  992.1 4.0 collective-permute-done
  996.8 14.4 %conditional.2 = (bf16[16,6144]{1,0:T(8,128)(2,1)}, bf16[16,48,128]{2,0,1:T(8,128)(2,1)}, bf16[16,64]{1,0:T(8,128)(2,1)S(1)}, bf16[16,64]{1,0:T(8,128)(2,1)}) conditional(s32[]{:T(128)} %convert_element_type.80, () %tuple.65, (pred[]{:T(512)}, bf16[192,6144]{1,0:T(8,128)(2,1)}, s32[]{:T(128)}, bf16[16,6144]{1,0:T(8,128)(2,1)}, s32[48]{0:T(128)}, ...), branch_computations={%region_3.3_spmd, %region_4.4_spmd} | conditional | flops 102634336 | bytes 17349906 | solution.py:116
  1018.0 5.3 collective-permute-done
  1024.0 14.4 %conditional.2 = (bf16[16,6144]{1,0:T(8,128)(2,1)}, bf16[16,48,128]{2,0,1:T(8,128)(2,1)}, bf16[16,64]{1,0:T(8,128)(2,1)S(1)}, bf16[16,64]{1,0:T(8,128)(2,1)}) conditional(s32[]{:T(128)} %convert_element_type.80, () %tuple.65, (pred[]{:T(512)}, bf16[192,6144]{1,0:T(8,128)(2,1)}, s32[]{:T(128)}, bf16[16,6144]{1,0:T(8,128)(2,1)}, s32[48]{0:T(128)}, ...), branch_computations={%region_3.3_spmd, %region_4.4_spmd} | conditional | flops 102634336 | bytes 17349906 | solution.py:116
  1045.2 5.5 collective-permute-done
  1051.4 14.4 %conditional.2 = (bf16[16,6144]{1,0:T(8,128)(2,1)}, bf16[16,48,128]{2,0,1:T(8,128)(2,1)}, bf16[16,64]{1,0:T(8,128)(2,1)S(1)}, bf16[16,64]{1,0:T(8,128)(2,1)}) conditional(s32[]{:T(128)} %convert_element_type.80, () %tuple.65, (pred[]{:T(512)}, bf16[192,6144]{1,0:T(8,128)(2,1)}, s32[]{:T(128)}, bf16[16,6144]{1,0:T(8,128)(2,1)}, s32[48]{0:T(128)}, ...), branch_computations={%region_3.3_spmd, %region_4.4_spmd} | conditional | flops 102634336 | bytes 17349906 | solution.py:116
  1072.6 7.1 collective-permute-done
  1080.4 14.4 %conditional.2 = (bf16[16,6144]{1,0:T(8,128)(2,1)}, bf16[16,48,128]{2,0,1:T(8,128)(2,1)}, bf16[16,64]{1,0:T(8,128)(2,1)S(1)}, bf16[16,64]{1,0:T(8,128)(2,1)}) conditional(s32[]{:T(128)} %convert_element_type.80, () %tuple.65, (pred[]{:T(512)}, bf16[192,6144]{1,0:T(8,128)(2,1)}, s32[]{:T(128)}, bf16[16,6144]{1,0:T(8,128)(2,1)}, s32[48]{0:T(128)}, ...), branch_computations={%region_3.3_spmd, %region_4.4_spmd} | conditional | flops 102634336 | bytes 17349906 | solution.py:116
  1101.6 13.1 collective-permute-done
  1115.3 14.4 %conditional.2 = (bf16[16,6144]{1,0:T(8,128)(2,1)}, bf16[16,48,128]{2,0,1:T(8,128)(2,1)}, bf16[16,64]{1,0:T(8,128)(2,1)S(1)}, bf16[16,64]{1,0:T(8,128)(2,1)}) conditional(s32[]{:T(128)} %convert_element_type.80, () %tuple.65, (pred[]{:T(512)}, bf16[192,6144]{1,0:T(8,128)(2,1)}, s32[]{:T(128)}, bf16[16,6144]{1,0:T(8,128)(2,1)}, s32[48]{0:T(128)}, ...), branch_computations={%region_3.3_spmd, %region_4.4_spmd} | conditional | flops 102634336 | bytes 17349906 | solution.py:116
  1136.5 5.4 collective-permute-done
  1142.6 14.3 %conditional.2 = (bf16[16,6144]{1,0:T(8,128)(2,1)}, bf16[16,48,128]{2,0,1:T(8,128)(2,1)}, bf16[16,64]{1,0:T(8,128)(2,1)S(1)}, bf16[16,64]{1,0:T(8,128)(2,1)}) conditional(s32[]{:T(128)} %convert_element_type.80, () %tuple.65, (pred[]{:T(512)}, bf16[192,6144]{1,0:T(8,128)(2,1)}, s32[]{:T(128)}, bf16[16,6144]{1,0:T(8,128)(2,1)}, s32[48]{0:T(128)}, ...), branch_computations={%region_3.3_spmd, %region_4.4_spmd} | conditional | flops 102634336 | bytes 17349906 | solution.py:116
  1167.4 14.2 %collective-permute-start = (bf16[16,6144]{1,0:T(8,128)(2,1)}, bf16[16,6144]{1,0:T(8,128)(2,1)S(1)}, u32[]{:S(2)}, u32[]{:S(2)}) collective-permute-start(bf16[16,6144]{1,0:T(8,128)(2,1)} %get-tuple-element.597), channel_id=1, source_target_pairs={{16,0},{32,16},{48,32},{64,48},{80,64},{96,80},{112,96},{128,112},... | collective-permute-start | bytes 589832 | tf_op jit(solution)/shard_map/while/body/eval_jaxpr/ppermute | solution.py:11
  1200.5 51.9 %reduce-scatter.12.cloned.1.call-done = bf16[384,64]{1,0:T(8,128)(2,1)} async-done(((bf16[6144,64]{1,0:T(8,128)(2,1)}), bf16[384,64]{1,0:T(8,128)(2,1)}) %reduce-scatter.12.cloned.1.call-update) | async-done | bytes 49168
  1254.0 67.6 %reduce-scatter.10.cloned.1.call-done = bf16[384,64]{1,0:T(8,128)(2,1)} async-done(((bf16[6144,64]{1,0:T(8,128)(2,1)}), bf16[384,64]{1,0:T(8,128)(2,1)}) %reduce-scatter.10.cloned.1.call-update) | async-done | bytes 49168
  1323.2 67.9 %reduce-scatter.8.cloned.1.call-done = bf16[3,128,128]{1,2,0:T(8,128)(2,1)} async-done(((bf16[48,128,128]{1,2,0:T(8,128)(2,1)}), bf16[3,128,128]{1,2,0:T(8,128)(2,1)}) %reduce-scatter.8.cloned.1.call-update) | async-done | bytes 98320 | tf_op jit(solution)/shard_map/reduce_scatter | solution.py:135
  (798 shorter events, 687.1 us)
Async XLA Ops:
  7.2 102.3 %all-gather.6.cloned.1.call-start = ((), (), s32[]{:S(2)}) async-start(), calls=%async_computation.3 | async-start | bytes 3244032 | tf_op jit(solution)/shard_map/all_gather | solution.py:74
  8.9 137.8 %all-gather.8.cloned.1.call-start = ((), (), s32[]{:S(2)}) async-start(), calls=%async_computation.5 | async-start | bytes 1671168 | tf_op jit(solution)/shard_map/all_gather | solution.py:70
  9.6 1242.8 %reduce-scatter.12.cloned.1.call-start = ((), (), s32[]{:S(2)}) async-start(), calls=%async_computation.7 | async-start | bytes 1671168
  154.3 9.1 collective-permute-start
  166.1 8.3 collective-permute-start
  177.1 8.4 collective-permute-start
  188.2 8.5 collective-permute-start
  199.4 9.0 collective-permute-start
  211.1 9.0 collective-permute-start
  222.7 9.0 collective-permute-start
  234.4 9.0 collective-permute-start
  246.1 12.7 collective-permute-start
  261.5 11.6 collective-permute-start
  275.8 10.1 collective-permute-start
  288.6 12.5 collective-permute-start
  303.8 12.8 collective-permute-start
  319.3 12.2 collective-permute-start
  334.3 11.8 collective-permute-start
  348.8 11.8 collective-permute-start
  363.3 10.3 collective-permute-start
  376.3 10.5 collective-permute-start
  389.5 10.8 collective-permute-start
  402.9 11.2 collective-permute-start
  416.8 13.2 collective-permute-start
  432.7 15.5 %collective-permute-start = (bf16[16,6144]{1,0:T(8,128)(2,1)}, bf16[16,6144]{1,0:T(8,128)(2,1)S(1)}, u32[]{:S(2)}, u32[]{:S(2)}) collective-permute-start(bf16[16,6144]{1,0:T(8,128)(2,1)} %get-tuple-element.597), channel_id=1, source_target_pairs={{16,0},{32,16},{48,32},{64,48},{80,64},{96,80},{112,96},{128,112},... | collective-permute-start | bytes 589832 | tf_op jit(solution)/shard_map/while/body/eval_jaxpr/ppermute | solution.py:11
  450.9 14.4 %collective-permute-start = (bf16[16,6144]{1,0:T(8,128)(2,1)}, bf16[16,6144]{1,0:T(8,128)(2,1)S(1)}, u32[]{:S(2)}, u32[]{:S(2)}) collective-permute-start(bf16[16,6144]{1,0:T(8,128)(2,1)} %get-tuple-element.597), channel_id=1, source_target_pairs={{16,0},{32,16},{48,32},{64,48},{80,64},{96,80},{112,96},{128,112},... | collective-permute-start | bytes 589832 | tf_op jit(solution)/shard_map/while/body/eval_jaxpr/ppermute | solution.py:11
  468.0 11.8 collective-permute-start
  482.5 10.3 collective-permute-start
  495.6 11.7 collective-permute-start
  509.9 10.4 collective-permute-start
  523.0 9.0 collective-permute-start
  534.7 9.0 collective-permute-start
  546.4 278.8 %collective-permute-start = (bf16[16,6144]{1,0:T(8,128)(2,1)}, bf16[16,6144]{1,0:T(8,128)(2,1)S(1)}, u32[]{:S(2)}, u32[]{:S(2)}) collective-permute-start(bf16[16,6144]{1,0:T(8,128)(2,1)} %get-tuple-element.597), channel_id=1, source_target_pairs={{16,0},{32,16},{48,32},{64,48},{80,64},{96,80},{112,96},{128,112},... | collective-permute-start | bytes 589832 | tf_op jit(solution)/shard_map/while/body/eval_jaxpr/ppermute | solution.py:11
  840.3 12.6 collective-permute-start
  868.0 13.1 collective-permute-start
  896.2 15.1 %collective-permute-start = (bf16[16,6144]{1,0:T(8,128)(2,1)}, bf16[16,6144]{1,0:T(8,128)(2,1)S(1)}, u32[]{:S(2)}, u32[]{:S(2)}) collective-permute-start(bf16[16,6144]{1,0:T(8,128)(2,1)} %get-tuple-element.597), channel_id=1, source_target_pairs={{16,0},{32,16},{48,32},{64,48},{80,64},{96,80},{112,96},{128,112},... | collective-permute-start | bytes 589832 | tf_op jit(solution)/shard_map/while/body/eval_jaxpr/ppermute | solution.py:11
  926.4 15.1 %collective-permute-start = (bf16[16,6144]{1,0:T(8,128)(2,1)}, bf16[16,6144]{1,0:T(8,128)(2,1)S(1)}, u32[]{:S(2)}, u32[]{:S(2)}) collective-permute-start(bf16[16,6144]{1,0:T(8,128)(2,1)} %get-tuple-element.597), channel_id=1, source_target_pairs={{16,0},{32,16},{48,32},{64,48},{80,64},{96,80},{112,96},{128,112},... | collective-permute-start | bytes 589832 | tf_op jit(solution)/shard_map/while/body/eval_jaxpr/ppermute | solution.py:11
  956.6 13.6 collective-permute-start
  985.4 10.7 collective-permute-start
  1011.2 12.1 collective-permute-start
  1038.5 12.2 collective-permute-start
  1065.8 13.8 collective-permute-start
  1094.8 19.8 %collective-permute-start = (bf16[16,6144]{1,0:T(8,128)(2,1)}, bf16[16,6144]{1,0:T(8,128)(2,1)S(1)}, u32[]{:S(2)}, u32[]{:S(2)}) collective-permute-start(bf16[16,6144]{1,0:T(8,128)(2,1)} %get-tuple-element.597), channel_id=1, source_target_pairs={{16,0},{32,16},{48,32},{64,48},{80,64},{96,80},{112,96},{128,112},... | collective-permute-start | bytes 589832 | tf_op jit(solution)/shard_map/while/body/eval_jaxpr/ppermute | solution.py:11
  1129.7 12.2 collective-permute-start
  1156.9 7.8 collective-permute-start
  1167.4 18.9 %collective-permute-start = (bf16[16,6144]{1,0:T(8,128)(2,1)}, bf16[16,6144]{1,0:T(8,128)(2,1)S(1)}, u32[]{:S(2)}, u32[]{:S(2)}) collective-permute-start(bf16[16,6144]{1,0:T(8,128)(2,1)} %get-tuple-element.597), channel_id=1, source_target_pairs={{16,0},{32,16},{48,32},{64,48},{80,64},{96,80},{112,96},{128,112},... | collective-permute-start | bytes 589832 | tf_op jit(solution)/shard_map/while/body/eval_jaxpr/ppermute | solution.py:11
  1191.8 129.8 %reduce-scatter.10.cloned.1.call-start = ((), (), s32[]{:S(2)}) async-start(), calls=%async_computation.6 | async-start | bytes 1671168
  1195.7 195.4 %reduce-scatter.8.cloned.1.call-start = ((), (), s32[]{:S(2)}) async-start(), calls=%async_computation.4 | async-start | bytes 1671168 | tf_op jit(solution)/shard_map/reduce_scatter | solution.py:135
  (119 other events, 262.4 us)
Sparse Core Ops, SparseCore 0:
  11.7 97.7 all-gather.5
  111.6 35.0 all-gather.7
  1191.9 60.4 reduce-scatter.11
  1255.1 66.4 reduce-scatter.9
  1324.3 66.7 reduce-scatter.7
where the time goes:
time: 1410 us; the launch traced here: 1400 us
  waiting for transfers between devices  729 us (52%)
  other arithmetic  237 us (17%)
  local copies, waits for them, and re-layouts  150 us (11%)
  matrix products  120 us (9%)
  starting transfers between devices  96.1 us (7%)
  blocking collectives  52.8 us (4%)
    ppermute x43, waiting for transfers between devices, shifted(): return lax.ppermute(shard, axis, pairs)  470 us
    dynamic_update_slice x129, other arithmetic, replace_rows(): lax.dynamic_update_slice_in_dim(buffer, jnp.where(active, fresh, older),...  203 us
    unnamed x7, waiting for transfers between devices  120 us
    ppermute x43, starting transfers between devices, shifted(): return lax.ppermute(shard, axis, pairs)  95.9 us
    reduce_scatter x1, waiting for transfers between devices, body(): lax.psum_scatter(grad_blocks.astype(jnp.bfloat16), 'dp', scatter_dimensio...  67.9 us
    another operation x128, local copies, waits for them, and re-layouts  65.9 us
    all_gather x1, waiting for transfers between devices, body(): head = lax.all_gather(loss_grad, 'pipe', axis=1, tiled=True)  41.7 us
    while x86, local copies, waits for them, and re-layouts  29.6 us
  transfers between devices with their start and end apart: 48, of which 47 were waited for; matrix products, arithmetic and copies ran while one was open for 16% of the time, Pallas kernels for 0%

commit v1 on v0

--- a/solution.py
+++ b/solution.py
@@ -71,7 +71,9 @@
         lax.all_gather(left_factor[0], "dp", axis=0, tiled=True),
         lax.all_gather(right_factor[0], "dp", axis=1, tiled=True),
     )
-    head = lax.all_gather(loss_grad, "pipe", axis=1, tiled=True)
+    head = jnp.concatenate(
+        lax.all_to_all(jnp.stack([loss_grad] * lax.axis_size("pipe")), "pipe", 0, 0), axis=1
+    )
     columns = block_column[0]
     inverse = inverse_of(columns)
     sections = lax.axis_size("pipe")

time: 1410 us -> 1420 us (level)
  waiting for transfers between devices: 729 us -> 652 us
  blocking collectives: 52.8 us -> 124 us
  starting transfers between devices: 96.1 us -> 116 us
    all_gather x1, blocking collectives: 29.2 us -> 102 us  [body(): lax.all_gather(left_factor[0], 'dp', axis=0, tiled=True)]
    all_gather x1 -> x0, waiting for transfers between devices: 41.7 us -> none  [body(): head = lax.all_gather(loss_grad, 'pipe', axis=1, tiled=True)]
    all_gather x1, waiting for transfers between devices: 28.8 us -> 0.01 us  [body(): lax.all_gather(weight_blocks[0], 'dp', axis=0, tiled=True)]
    all_to_all x0 -> x1, starting transfers between devices: none -> 16.3 us  [body(): lax.all_to_all(jnp.stack([loss_grad] * lax.axis_size('pipe')), 'pipe', 0, 0)]
    ppermute x43, waiting for transfers between devices: 470 us -> 455 us  [shifted(): return lax.ppermute(shard, axis, pairs)]
    unnamed x7 -> x6, waiting for transfers between devices: 120 us -> 129 us
    while x87 -> x86, local copies, waits for them, and re-layouts: 34.3 us -> 30 us
    another operation x128 -> x129, local copies, waits for them, and re-layouts: 65.9 us -> 67.9 us
  transfers between devices with their start and end apart: 48 -> 48, of which waited for: 47 -> 45; matrix products, arithmetic and copies ran while one was open for 16% -> 16% of each run, Pallas kernels for 0% -> 0%
where the time goes in v1:
time: 1420 us
  waiting for transfers between devices  652 us (46%)
  other arithmetic  236 us (17%)
  local copies, waits for them, and re-layouts  156 us (11%)
  blocking collectives  124 us (9%)
  matrix products  118 us (8%)
  starting transfers between devices  116 us (8%)
    ppermute x43, waiting for transfers between devices, shifted(): return lax.ppermute(shard, axis, pairs)  455 us
    dynamic_update_slice x129, other arithmetic, replace_rows(): lax.dynamic_update_slice_in_dim(buffer, jnp.where(active, fresh, older),...  203 us
    unnamed x6, waiting for transfers between devices  129 us
    all_gather x1, blocking collectives, body(): lax.all_gather(left_factor[0], 'dp', axis=0, tiled=True)  102 us
    ppermute x43, starting transfers between devices, shifted(): return lax.ppermute(shard, axis, pairs)  99.8 us
    reduce_scatter x1, waiting for transfers between devices, body(): lax.psum_scatter(grad_blocks.astype(jnp.bfloat16), 'dp', scatter_dimensio...  67.9 us
    another operation x128, local copies, waits for them, and re-layouts  65 us
    while x86, local copies, waits for them, and re-layouts  30 us
  transfers between devices with their start and end apart: 48, of which 45 were waited for; matrix products, arithmetic and copies ran while one was open for 16% of the time, Pallas kernels for 0%

profile of v1, /device:TPU:8, one launch (start us, length us, event | category | flops | bytes accessed | tf_op | source)
XLA Modules:
  0.0 1417.4 jit_solution(12830151404134178841)
XLA Ops:
  10.1 16.3 %all-to-all-start = ((bf16[32,192,192]{2,1,0:T(8,128)(2,1)}), bf16[32,192,192]{2,1,0:T(8,128)(2,1)}, u32[]{:S(2)}, u32[]{:S(2)}) async-start(bf16[32,192,192]{2,1,0:T(8,128)(2,1)} %stack.2), calls=%async_computation | async-start | bytes 6291456 | tf_op jit(solution)/shard_map/all_to_all | solution.py:75
  31.2 102.1 %all-gather.1 = bf16[1,6144,64]{2,1,0:T(8,128)(2,1)S(1)} all-gather(bf16[1,384,64]{2,1,0:T(8,128)(2,1)S(1)} %copy.52), channel_id=3, replica_groups=mesh['pipe'=32,'dp'=16] {'dp'}, dimensions={1}, use_global_device_ids=true | all-gather | bytes 835584 | tf_op jit(solution)/shard_map/all_gather | solution.py:71
  133.3 22.1 %all-gather.2 = bf16[1,64,6144]{2,1,0:T(8,128)(2,1)} all-gather(bf16[1,64,384]{2,1,0:T(8,128)(2,1)S(1)} %copy-done.11), channel_id=4, replica_groups=mesh['pipe'=32,'dp'=16] {'dp'}, dimensions={2}, use_global_device_ids=true | all-gather | bytes 835584 | tf_op jit(solution)/shard_map/all_gather | solution.py:72
  155.4 5.3 copy.50
  160.8 6.2 reshape.96
  175.9 1022.5 %while.23 = (s32[]{:T(128)}, bf16[16,6144]{1,0:T(8,128)(2,1)}, bf16[192,6144]{1,0:T(8,128)(2,1)}, bf16[192,48,128]{2,0,1:T(8,128)(2,1)}, bf16[192,64]{1,0:T(8,12...) while((s32[]{:T(128)}, bf16[16,6144]{1,0:T(8,128)(2,1)}, ...), condition=%wide.region_5.6_spmd, body=%wide.region_2.5_spmd.sunk | while | flops 102833008 | bytes 20126928 | solution.py:131
  277.7 4.7 collective-permute-done
  291.7 9.8 collective-permute-done
  310.8 6.4 collective-permute-done
  326.4 5.8 collective-permute-done
  341.4 5.3 collective-permute-done
  356.0 4.2 collective-permute-done
  394.2 6.4 collective-permute-done
  409.9 5.4 collective-permute-done
  437.7 4.3 collective-permute-done
  477.0 4.3 collective-permute-done
  490.6 5.5 collective-permute-done
  505.4 8.3 collective-permute-done
  522.9 5.9 collective-permute-done
  538.1 4.8 collective-permute-done
  575.3 270.2 %collective-permute-done = bf16[16,6144]{1,0:T(8,128)(2,1)S(1)} collective-permute-done((bf16[16,6144]{1,0:T(8,128)(2,1)}, bf16[16,6144]{1,0:T(8,128)(2,1)S(1)}, u32[]{:S(2)}, u32[]{:S(2)}) %collective-permute-start) | collective-permute-done | bytes 196640 | tf_op jit(solution)/shard_map/while/body/eval_jaxpr/ppermute | solution.py:11
  846.1 14.4 %conditional.2 = (bf16[16,6144]{1,0:T(8,128)(2,1)}, bf16[16,48,128]{2,0,1:T(8,128)(2,1)}, bf16[16,64]{1,0:T(8,128)(2,1)S(1)}, bf16[16,64]{1,0:T(8,128)(2,1)}) conditional(s32[]{:T(128)} %convert_element_type.80, () %tuple.64, (pred[]{:T(512)}, bf16[192,6144]{1,0:T(8,128)(2,1)}, s32[]{:T(128)}, bf16[16,6144]{1,0:T(8,128)(2,1)}, s32[48]{0:T(128)}, ...), branch_computations={%region_3.3_spmd, %region_4.4_spmd} | conditional | flops 102634336 | bytes 17349906 | solution.py:118
  867.3 10.2 collective-permute-done
  878.2 14.4 %conditional.2 = (bf16[16,6144]{1,0:T(8,128)(2,1)}, bf16[16,48,128]{2,0,1:T(8,128)(2,1)}, bf16[16,64]{1,0:T(8,128)(2,1)S(1)}, bf16[16,64]{1,0:T(8,128)(2,1)}) conditional(s32[]{:T(128)} %convert_element_type.80, () %tuple.64, (pred[]{:T(512)}, bf16[192,6144]{1,0:T(8,128)(2,1)}, s32[]{:T(128)}, bf16[16,6144]{1,0:T(8,128)(2,1)}, s32[48]{0:T(128)}, ...), branch_computations={%region_3.3_spmd, %region_4.4_spmd} | conditional | flops 102634336 | bytes 17349906 | solution.py:118
  899.4 6.8 collective-permute-done
  906.8 14.4 %conditional.2 = (bf16[16,6144]{1,0:T(8,128)(2,1)}, bf16[16,48,128]{2,0,1:T(8,128)(2,1)}, bf16[16,64]{1,0:T(8,128)(2,1)S(1)}, bf16[16,64]{1,0:T(8,128)(2,1)}) conditional(s32[]{:T(128)} %convert_element_type.80, () %tuple.64, (pred[]{:T(512)}, bf16[192,6144]{1,0:T(8,128)(2,1)}, s32[]{:T(128)}, bf16[16,6144]{1,0:T(8,128)(2,1)}, s32[48]{0:T(128)}, ...), branch_computations={%region_3.3_spmd, %region_4.4_spmd} | conditional | flops 102634336 | bytes 17349906 | solution.py:118
  928.0 6.1 collective-permute-done
  934.8 14.4 %conditional.2 = (bf16[16,6144]{1,0:T(8,128)(2,1)}, bf16[16,48,128]{2,0,1:T(8,128)(2,1)}, bf16[16,64]{1,0:T(8,128)(2,1)S(1)}, bf16[16,64]{1,0:T(8,128)(2,1)}) conditional(s32[]{:T(128)} %convert_element_type.80, () %tuple.64, (pred[]{:T(512)}, bf16[192,6144]{1,0:T(8,128)(2,1)}, s32[]{:T(128)}, bf16[16,6144]{1,0:T(8,128)(2,1)}, s32[48]{0:T(128)}, ...), branch_computations={%region_3.3_spmd, %region_4.4_spmd} | conditional | flops 102634336 | bytes 17349906 | solution.py:118
  956.0 5.4 collective-permute-done
  962.1 14.4 %conditional.2 = (bf16[16,6144]{1,0:T(8,128)(2,1)}, bf16[16,48,128]{2,0,1:T(8,128)(2,1)}, bf16[16,64]{1,0:T(8,128)(2,1)S(1)}, bf16[16,64]{1,0:T(8,128)(2,1)}) conditional(s32[]{:T(128)} %convert_element_type.80, () %tuple.64, (pred[]{:T(512)}, bf16[192,6144]{1,0:T(8,128)(2,1)}, s32[]{:T(128)}, bf16[16,6144]{1,0:T(8,128)(2,1)}, s32[48]{0:T(128)}, ...), branch_computations={%region_3.3_spmd, %region_4.4_spmd} | conditional | flops 102634336 | bytes 17349906 | solution.py:118
  983.2 4.2 collective-permute-done
  988.1 14.4 %conditional.2 = (bf16[16,6144]{1,0:T(8,128)(2,1)}, bf16[16,48,128]{2,0,1:T(8,128)(2,1)}, bf16[16,64]{1,0:T(8,128)(2,1)S(1)}, bf16[16,64]{1,0:T(8,128)(2,1)}) conditional(s32[]{:T(128)} %convert_element_type.80, () %tuple.64, (pred[]{:T(512)}, bf16[192,6144]{1,0:T(8,128)(2,1)}, s32[]{:T(128)}, bf16[16,6144]{1,0:T(8,128)(2,1)}, s32[48]{0:T(128)}, ...), branch_computations={%region_3.3_spmd, %region_4.4_spmd} | conditional | flops 102634336 | bytes 17349906 | solution.py:118
  1009.3 4.7 collective-permute-done
  1014.6 14.4 %conditional.2 = (bf16[16,6144]{1,0:T(8,128)(2,1)}, bf16[16,48,128]{2,0,1:T(8,128)(2,1)}, bf16[16,64]{1,0:T(8,128)(2,1)S(1)}, bf16[16,64]{1,0:T(8,128)(2,1)}) conditional(s32[]{:T(128)} %convert_element_type.80, () %tuple.64, (pred[]{:T(512)}, bf16[192,6144]{1,0:T(8,128)(2,1)}, s32[]{:T(128)}, bf16[16,6144]{1,0:T(8,128)(2,1)}, s32[48]{0:T(128)}, ...), branch_computations={%region_3.3_spmd, %region_4.4_spmd} | conditional | flops 102634336 | bytes 17349906 | solution.py:118
  1035.8 7.6 collective-permute-done
  1044.1 14.4 %conditional.2 = (bf16[16,6144]{1,0:T(8,128)(2,1)}, bf16[16,48,128]{2,0,1:T(8,128)(2,1)}, bf16[16,64]{1,0:T(8,128)(2,1)S(1)}, bf16[16,64]{1,0:T(8,128)(2,1)}) conditional(s32[]{:T(128)} %convert_element_type.80, () %tuple.64, (pred[]{:T(512)}, bf16[192,6144]{1,0:T(8,128)(2,1)}, s32[]{:T(128)}, bf16[16,6144]{1,0:T(8,128)(2,1)}, s32[48]{0:T(128)}, ...), branch_computations={%region_3.3_spmd, %region_4.4_spmd} | conditional | flops 102634336 | bytes 17349906 | solution.py:118
  1065.2 7.0 collective-permute-done
  1073.0 14.4 %conditional.2 = (bf16[16,6144]{1,0:T(8,128)(2,1)}, bf16[16,48,128]{2,0,1:T(8,128)(2,1)}, bf16[16,64]{1,0:T(8,128)(2,1)S(1)}, bf16[16,64]{1,0:T(8,128)(2,1)}) conditional(s32[]{:T(128)} %convert_element_type.80, () %tuple.64, (pred[]{:T(512)}, bf16[192,6144]{1,0:T(8,128)(2,1)}, s32[]{:T(128)}, bf16[16,6144]{1,0:T(8,128)(2,1)}, s32[48]{0:T(128)}, ...), branch_computations={%region_3.3_spmd, %region_4.4_spmd} | conditional | flops 102634336 | bytes 17349906 | solution.py:118
  1094.1 5.5 collective-permute-done
  1100.4 14.4 %conditional.2 = (bf16[16,6144]{1,0:T(8,128)(2,1)}, bf16[16,48,128]{2,0,1:T(8,128)(2,1)}, bf16[16,64]{1,0:T(8,128)(2,1)S(1)}, bf16[16,64]{1,0:T(8,128)(2,1)}) conditional(s32[]{:T(128)} %convert_element_type.80, () %tuple.64, (pred[]{:T(512)}, bf16[192,6144]{1,0:T(8,128)(2,1)}, s32[]{:T(128)}, bf16[16,6144]{1,0:T(8,128)(2,1)}, s32[48]{0:T(128)}, ...), branch_computations={%region_3.3_spmd, %region_4.4_spmd} | conditional | flops 102634336 | bytes 17349906 | solution.py:118
  1121.5 5.3 collective-permute-done
  1127.6 14.4 %conditional.2 = (bf16[16,6144]{1,0:T(8,128)(2,1)}, bf16[16,48,128]{2,0,1:T(8,128)(2,1)}, bf16[16,64]{1,0:T(8,128)(2,1)S(1)}, bf16[16,64]{1,0:T(8,128)(2,1)}) conditional(s32[]{:T(128)} %convert_element_type.80, () %tuple.64, (pred[]{:T(512)}, bf16[192,6144]{1,0:T(8,128)(2,1)}, s32[]{:T(128)}, bf16[16,6144]{1,0:T(8,128)(2,1)}, s32[48]{0:T(128)}, ...), branch_computations={%region_3.3_spmd, %region_4.4_spmd} | conditional | flops 102634336 | bytes 17349906 | solution.py:118
  1148.7 4.8 collective-permute-done
  1154.2 14.2 %conditional.2 = (bf16[16,6144]{1,0:T(8,128)(2,1)}, bf16[16,48,128]{2,0,1:T(8,128)(2,1)}, bf16[16,64]{1,0:T(8,128)(2,1)S(1)}, bf16[16,64]{1,0:T(8,128)(2,1)}) conditional(s32[]{:T(128)} %convert_element_type.80, () %tuple.64, (pred[]{:T(512)}, bf16[192,6144]{1,0:T(8,128)(2,1)}, s32[]{:T(128)}, bf16[16,6144]{1,0:T(8,128)(2,1)}, s32[48]{0:T(128)}, ...), branch_computations={%region_3.3_spmd, %region_4.4_spmd} | conditional | flops 102634336 | bytes 17349906 | solution.py:118
  1178.9 14.2 %collective-permute-start = (bf16[16,6144]{1,0:T(8,128)(2,1)}, bf16[16,6144]{1,0:T(8,128)(2,1)S(1)}, u32[]{:S(2)}, u32[]{:S(2)}) collective-permute-start(bf16[16,6144]{1,0:T(8,128)(2,1)} %get-tuple-element.571), channel_id=1, source_target_pairs={{16,0},{32,16},{48,32},{64,48},{80,64},{96,80},{112,96},{128,112},... | collective-permute-start | bytes 589832 | tf_op jit(solution)/shard_map/while/body/eval_jaxpr/ppermute | solution.py:11
  1210.2 59.9 %reduce-scatter.12.cloned.1.call-done = bf16[384,64]{1,0:T(8,128)(2,1)} async-done(((bf16[6144,64]{1,0:T(8,128)(2,1)}), bf16[384,64]{1,0:T(8,128)(2,1)}) %reduce-scatter.12.cloned.1.call-update) | async-done | bytes 49168
  1271.6 68.0 %reduce-scatter.10.cloned.1.call-done = bf16[384,64]{1,0:T(8,128)(2,1)} async-done(((bf16[6144,64]{1,0:T(8,128)(2,1)}), bf16[384,64]{1,0:T(8,128)(2,1)}) %reduce-scatter.10.cloned.1.call-update) | async-done | bytes 49168
  1341.3 67.9 %reduce-scatter.8.cloned.1.call-done = bf16[3,128,128]{1,2,0:T(8,128)(2,1)} async-done(((bf16[48,128,128]{1,2,0:T(8,128)(2,1)}), bf16[3,128,128]{1,2,0:T(8,128)(2,1)}) %reduce-scatter.8.cloned.1.call-update) | async-done | bytes 98320 | tf_op jit(solution)/shard_map/reduce_scatter | solution.py:137
  (806 shorter events, 682.4 us)
Async XLA Ops:
  10.1 145.3 %all-to-all-start = ((bf16[32,192,192]{2,1,0:T(8,128)(2,1)}), bf16[32,192,192]{2,1,0:T(8,128)(2,1)}, u32[]{:S(2)}, u32[]{:S(2)}) async-start(bf16[32,192,192]{2,1,0:T(8,128)(2,1)} %stack.2), calls=%async_computation | async-start | bytes 6291456 | tf_op jit(solution)/shard_map/all_to_all | solution.py:75
  26.5 143.8 %all-gather.5.cloned.1.call-start = ((), (), s32[]{:S(2)}) async-start(), calls=%async_computation.5 | async-start | bytes 1671168 | tf_op jit(solution)/shard_map/all_gather | solution.py:70
  27.2 1242.8 %reduce-scatter.12.cloned.1.call-start = ((), (), s32[]{:S(2)}) async-start(), calls=%async_computation.7 | async-start | bytes 1671168
  177.9 9.2 collective-permute-start
  189.8 9.5 collective-permute-start
  202.0 8.7 collective-permute-start
  213.4 8.4 collective-permute-start
  224.5 8.9 collective-permute-start
  236.1 9.0 collective-permute-start
  247.8 9.0 collective-permute-start
  259.4 9.0 collective-permute-start
  271.1 11.3 collective-permute-start
  285.1 16.4 %collective-permute-start = (bf16[16,6144]{1,0:T(8,128)(2,1)}, bf16[16,6144]{1,0:T(8,128)(2,1)S(1)}, u32[]{:S(2)}, u32[]{:S(2)}) collective-permute-start(bf16[16,6144]{1,0:T(8,128)(2,1)} %get-tuple-element.571), channel_id=1, source_target_pairs={{16,0},{32,16},{48,32},{64,48},{80,64},{96,80},{112,96},{128,112},... | collective-permute-start | bytes 589832 | tf_op jit(solution)/shard_map/while/body/eval_jaxpr/ppermute | solution.py:11
  304.2 12.9 collective-permute-start
  319.8 12.4 collective-permute-start
  334.9 11.9 collective-permute-start
  349.4 10.8 collective-permute-start
  362.9 9.8 collective-permute-start
  375.4 9.5 collective-permute-start
  387.6 13.0 collective-permute-start
  403.3 12.0 collective-permute-start
  417.9 10.5 collective-permute-start
  431.1 10.9 collective-permute-start
  444.7 10.5 collective-permute-start
  457.8 10.0 collective-permute-start
  470.4 10.9 collective-permute-start
  484.0 12.1 collective-permute-start
  498.8 14.9 %collective-permute-start = (bf16[16,6144]{1,0:T(8,128)(2,1)}, bf16[16,6144]{1,0:T(8,128)(2,1)S(1)}, u32[]{:S(2)}, u32[]{:S(2)}) collective-permute-start(bf16[16,6144]{1,0:T(8,128)(2,1)} %get-tuple-element.571), channel_id=1, source_target_pairs={{16,0},{32,16},{48,32},{64,48},{80,64},{96,80},{112,96},{128,112},... | collective-permute-start | bytes 589832 | tf_op jit(solution)/shard_map/while/body/eval_jaxpr/ppermute | solution.py:11
  516.3 12.5 collective-permute-start
  531.5 11.4 collective-permute-start
  545.6 7.8 collective-permute-start
  556.0 10.0 collective-permute-start
  568.7 276.8 %collective-permute-start = (bf16[16,6144]{1,0:T(8,128)(2,1)}, bf16[16,6144]{1,0:T(8,128)(2,1)S(1)}, u32[]{:S(2)}, u32[]{:S(2)}) collective-permute-start(bf16[16,6144]{1,0:T(8,128)(2,1)} %get-tuple-element.571), channel_id=1, source_target_pairs={{16,0},{32,16},{48,32},{64,48},{80,64},{96,80},{112,96},{128,112},... | collective-permute-start | bytes 589832 | tf_op jit(solution)/shard_map/while/body/eval_jaxpr/ppermute | solution.py:11
  860.5 17.0 %collective-permute-start = (bf16[16,6144]{1,0:T(8,128)(2,1)}, bf16[16,6144]{1,0:T(8,128)(2,1)S(1)}, u32[]{:S(2)}, u32[]{:S(2)}) collective-permute-start(bf16[16,6144]{1,0:T(8,128)(2,1)} %get-tuple-element.571), channel_id=1, source_target_pairs={{16,0},{32,16},{48,32},{64,48},{80,64},{96,80},{112,96},{128,112},... | collective-permute-start | bytes 589832 | tf_op jit(solution)/shard_map/while/body/eval_jaxpr/ppermute | solution.py:11
  892.6 13.5 collective-permute-start
  921.2 12.9 collective-permute-start
  949.2 12.2 collective-permute-start
  976.5 10.9 collective-permute-start
  1002.5 11.4 collective-permute-start
  1029.0 14.4 %collective-permute-start = (bf16[16,6144]{1,0:T(8,128)(2,1)}, bf16[16,6144]{1,0:T(8,128)(2,1)S(1)}, u32[]{:S(2)}, u32[]{:S(2)}) collective-permute-start(bf16[16,6144]{1,0:T(8,128)(2,1)} %get-tuple-element.571), channel_id=1, source_target_pairs={{16,0},{32,16},{48,32},{64,48},{80,64},{96,80},{112,96},{128,112},... | collective-permute-start | bytes 589832 | tf_op jit(solution)/shard_map/while/body/eval_jaxpr/ppermute | solution.py:11
  1058.5 13.8 collective-permute-start
  1087.4 12.3 collective-permute-start
  1114.7 12.1 collective-permute-start
  1141.9 11.6 collective-permute-start
  1168.5 7.8 collective-permute-start
  1178.9 18.8 %collective-permute-start = (bf16[16,6144]{1,0:T(8,128)(2,1)}, bf16[16,6144]{1,0:T(8,128)(2,1)S(1)}, u32[]{:S(2)}, u32[]{:S(2)}) collective-permute-start(bf16[16,6144]{1,0:T(8,128)(2,1)} %get-tuple-element.571), channel_id=1, source_target_pairs={{16,0},{32,16},{48,32},{64,48},{80,64},{96,80},{112,96},{128,112},... | collective-permute-start | bytes 589832 | tf_op jit(solution)/shard_map/while/body/eval_jaxpr/ppermute | solution.py:11
  1203.3 136.4 %reduce-scatter.10.cloned.1.call-start = ((), (), s32[]{:S(2)}) async-start(), calls=%async_computation.6 | async-start | bytes 1671168
  1206.1 203.1 %reduce-scatter.8.cloned.1.call-start = ((), (), s32[]{:S(2)}) async-start(), calls=%async_computation.4 | async-start | bytes 1671168 | tf_op jit(solution)/shard_map/reduce_scatter | solution.py:137
  (123 other events, 422.5 us)
Sparse Core Ops, SparseCore 0:
  29.4 92.9 all-gather.4
  1203.4 66.5 reduce-scatter.11
  1272.9 66.7 reduce-scatter.9
  1342.4 66.7 reduce-scatter.7
